TPU v7x, 256 devices: a whole 4x4x8 slice. The times are simulated.
256 devices in a mesh: outer: 8 (over z), inner: 32 (over y, x, core).
Axes of the slice: x: 4, y: 4, z: 8, core: 2. Of those that a mesh axis runs over, the one named last changes fastest.
Arguments:
- context: bfloat16 [32768, 4096], P(('outer', 'inner')), may hold values from -5 to 5
- query_acts: bfloat16 [64, 4096], replicated, may hold values from -5 to 5
- norm_gain: float32 [4096], replicated, may hold values from 0.25 to 1.75
- w_query: bfloat16 [4096, 2048], P('inner'), may hold values from -0.078125 to 0.078125
- w_key: bfloat16 [4096, 512], P('inner'), may hold values from -0.453125 to 0.453125
- value_weight: bfloat16 [4096, 512], P('inner'), may hold values from -0.09375 to 0.09375
- lengths: int32 [256], replicated, may hold values from 64 to 128, as said below
Outputs:
- block_out: bfloat16 [32768, 2048], P(('outer', 'inner'))
- query_out: bfloat16 [64, 2048], replicated
Inputs may be any that keep to these rules, and one draw needn't show every extreme that they name: `lengths`: valid tokens of a block are its first ones; the rest of it is padding.
All inputs are finite; a program needn't handle non-finite values.
Results may differ from a plain program's by a relative error of at most 0.004.
The roundings to bfloat16 on the way count: a program that leaves them out, or rounds other values in their place, can miss the bound.
Values may be sent and summed in bfloat16 or wider, within the bound.
No kernel may reach another device: no remote copies, remote signals or barrier semaphores. Data moves between devices by JAX's collectives and lax.ppermute only.
A program may use at most 320 MiB of HBM per device.

v0:
```python
import jax
import jax.numpy as jnp
from jax import lax
from jax.sharding import PartitionSpec as P

QUERY_HEADS = 16
KEY_VALUE_HEADS = 4
HEAD_SIZE = 128
epsilon = 1e-05


def broadcast(block, axis, owner):
    block = jnp.where(lax.axis_index(axis) == owner, block, jnp.zeros_like(block))
    return lax.psum(block, axis)


def normalize(matrix, norm_gain):
    widened = matrix.astype(jnp.float32)
    factor = lax.rsqrt(jnp.mean(widened * widened, axis=-1, keepdims=True) + epsilon)
    return (widened * factor * norm_gain).astype(jnp.bfloat16)


def attend_part(query_rows, key_row_block, value_matrix, allowed):
    count_of_rows = query_rows.shape[0]
    head_groups = query_rows.reshape(
        count_of_rows, KEY_VALUE_HEADS, QUERY_HEADS // KEY_VALUE_HEADS, HEAD_SIZE
    )
    per_head_keys = key_row_block.reshape(key_row_block.shape[0], KEY_VALUE_HEADS, HEAD_SIZE)
    per_head_values = value_matrix.reshape(value_matrix.shape[0], KEY_VALUE_HEADS, HEAD_SIZE)
    scores = jnp.einsum(
        "rhgd,khd->hgrk", head_groups, per_head_keys, preferred_element_type=jnp.float32
    ) * HEAD_SIZE ** (-0.5)
    scores = jnp.where(allowed, scores, -jnp.inf)
    maxima = jnp.max(scores, axis=-1)
    weights = jnp.exp(scores - maxima[..., None])
    sum_exp = jnp.sum(weights, axis=-1)
    numerator = jnp.einsum(
        "hgrk,khd->rhgd",
        weights.astype(jnp.bfloat16),
        per_head_values,
        preferred_element_type=jnp.float32,
    )
    return (
        maxima.reshape(QUERY_HEADS, count_of_rows),
        sum_exp.reshape(QUERY_HEADS, count_of_rows),
        numerator.reshape(count_of_rows, QUERY_HEADS * HEAD_SIZE),
    )


def spread(factor):
    return jnp.repeat(factor.T, HEAD_SIZE, axis=1)


def combine(former, latter):
    maxima = jnp.maximum(former[0], latter[0])
    scale_one = jnp.exp(former[0] - maxima)
    scale_two = jnp.exp(latter[0] - maxima)
    return (
        maxima,
        former[1] * scale_one + latter[1] * scale_two,
        former[2] * spread(scale_one) + latter[2] * spread(scale_two),
    )


def finish(pieces):
    return (pieces[2] / spread(pieces[1])).astype(jnp.bfloat16)


def share_anchor(stacked):
    return broadcast(stacked, ("outer", "inner"), 0)


def per_device(context, query_acts, norm_gain, w_query, w_key, value_weight, lengths):
    block_rows = context.shape[0]
    normed = jnp.concatenate(
        [normalize(context, norm_gain), normalize(query_acts, norm_gain)], axis=0
    )

    def apply_weight(whole_weight):
        return jnp.dot(normed, whole_weight, preferred_element_type=jnp.float32).astype(
            jnp.bfloat16
        )

    whole_q, whole_k, whole_v = (
        lax.all_gather(w_query, "inner", axis=0, tiled=True),
        lax.all_gather(w_key, "inner", axis=0, tiled=True),
        lax.all_gather(value_weight, "inner", axis=0, tiled=True),
    )
    projected_k = apply_weight(whole_k)
    projected_v = apply_weight(whole_v)
    anchor = share_anchor(jnp.stack([projected_k[:block_rows], projected_v[:block_rows]]))
    projected_q = apply_weight(whole_q)
    position = lax.axis_index(("outer", "inner"))
    own_length = lengths[position]
    anchor_length = lengths[0]
    places = jnp.arange(block_rows, dtype=jnp.int32)
    causal = places[:, None] >= places[None, :]
    block_q = projected_q[:block_rows]
    block_k = projected_k[:block_rows]
    block_v = projected_v[:block_rows]
    query_q = projected_q[block_rows:]
    query_k = projected_k[block_rows:]
    query_v = projected_v[block_rows:]
    query_count = query_q.shape[0]
    own_allowed = causal & (places[None, :] < own_length)
    anchor_allowed = jnp.broadcast_to(
        (places[None, :] < anchor_length) & (position > 0), (block_rows, block_rows)
    )
    allowed = jnp.concatenate([anchor_allowed, own_allowed], axis=1)
    key_row_block = jnp.concatenate([anchor[0], block_k], axis=0)
    value_rows = jnp.concatenate([anchor[1], block_v], axis=0)
    block_out = finish(attend_part(block_q, key_row_block, value_rows, allowed))
    reached = jnp.broadcast_to(places[None, :] < own_length, (query_count, block_rows))
    block_part = attend_part(query_q, block_k, block_v, reached)
    highest = lax.pmax(block_part[0], ("outer", "inner"))
    rescale = jnp.exp(block_part[0] - highest)
    summed_parts = lax.psum(
        (block_part[1] * rescale, block_part[2] * spread(rescale)), ("outer", "inner")
    )
    merged = (highest, summed_parts[0], summed_parts[1])
    query_places = jnp.arange(query_count, dtype=jnp.int32)
    self_part = attend_part(
        query_q, query_k, query_v, query_places[:, None] >= query_places[None, :]
    )
    return (block_out, finish(combine(merged, self_part)))


def solution(mesh):
    in_specs = (
        P(("outer", "inner"), None),
        P(),
        P(),
        P("inner", None),
        P("inner", None),
        P("inner", None),
        P(),
    )
    out_specs = (P(("outer", "inner"), None), P())
    return jax.shard_map(
        per_device, mesh=mesh, in_specs=in_specs, out_specs=out_specs, check_vma=False
    )
```

profile of v0, /device:TPU:2, one launch (start us, length us, event | category | flops | bytes accessed | tf_op | source)
XLA Modules:
  0.0 875.9 jit_solution(4082930749184454192)
XLA Ops:
  7.2 0.7 all-gather.4.cloned.1.call-update
  8.0 0.7 all-gather.6.cloned.1.call-update
  8.7 1.2 fusion.9
  10.0 1.5 fusion
  11.5 0.9 fusion.11
  12.5 0.3 fusion.2
  12.8 51.5 %all-gather.4.cloned.1.call-done = bf16[4096,512]{1,0:T(8,128)(2,1)} async-done(((bf16[128,512]{1,0:T(8,128)(2,1)}), bf16[4096,512]{1,0:T(8,128)(2,1)}) %all-gather.4.cloned.1.call-update) | async-done | bytes 4194320 | tf_op jit(solution)/shard_map/all_gather | solution.py:86
  64.3 3.2 convolution_convert_fusion.2
  67.6 49.9 %all-gather.6.cloned.1.call-done = bf16[4096,512]{1,0:T(8,128)(2,1)} async-done(((bf16[128,512]{1,0:T(8,128)(2,1)}), bf16[4096,512]{1,0:T(8,128)(2,1)}) %all-gather.6.cloned.1.call-update) | async-done | bytes 4194320 | tf_op jit(solution)/shard_map/all_gather | solution.py:87
  117.5 3.2 convolution_convert_fusion.1
  120.7 0.7 maximum_select_fusion
  121.5 0.5 all-gather.8.cloned.1.call-update
  122.1 0.6 fusion.52
  122.7 0.6 compare_and_fusion
  123.2 0.6 iota_compare_fusion.2
  124.1 0.8 copy.28
  124.9 0.7 concatenate.28
  125.6 0.6 reshape.106
  126.2 0.6 reshape.109
  126.9 246.7 %all-reduce.3.cloned.1.call-done = bf16[2,128,512]{2,1,0:T(8,128)(2,1)} async-done(((bf16[2,128,512]{2,1,0:T(8,128)(2,1)}), bf16[2,128,512]{2,1,0:T(8,128)(2,1)}) %all-reduce.3.cloned.1.call-update) | async-done | bytes 262160 | tf_op jit(solution)/shard_map/psum | solution.py:14
  373.5 1.0 fusion.49
  374.6 0.8 copy.56
  375.4 76.8 %all-gather.8.cloned.1.call-done = bf16[4096,2048]{1,0:T(8,128)(2,1)} async-done(((bf16[128,2048]{1,0:T(8,128)(2,1)}), bf16[4096,2048]{1,0:T(8,128)(2,1)}) %all-gather.8.cloned.1.call-update) | async-done | bytes 16777232 | tf_op jit(solution)/shard_map/all_gather | solution.py:85
  452.2 7.7 convolution_convert_fusion
  459.9 0.4 reshape.98
  460.3 0.5 fusion.53
  460.8 0.3 fusion.3
  461.2 0.5 fusion.12
  461.8 0.3 copy.34
  462.4 0.3 copy-done.9
  462.7 0.4 fusion.54
  463.1 76.0 %pmax.7 = f32[16,64]{1,0:T(8,128)S(1)} all-reduce(f32[16,64]{1,0:T(8,128)S(1)} %bitcast.97), channel_id=1, replica_groups=mesh['outer'=8,'inner'=32] {'outer','inner'}, use_global_device_ids=true, to_apply=%region_6.7 | all-reduce | flops 1024 | bytes 8192 | tf_op jit(solution)/shard_map/pmax | solution.py:115
  539.1 0.4 fusion.19
  539.5 74.4 %psum.23 = f32[16,64]{1,0:T(8,128)S(1)} all-reduce(f32[16,64]{1,0:T(8,128)S(1)} %get-tuple-element.13), channel_id=1, replica_groups=mesh['outer'=8,'inner'=32] {'outer','inner'}, use_global_device_ids=true, to_apply=%region_10.11 | all-reduce | flops 1024 | bytes 8192 | tf_op jit(solution)/shard_map/psum | solution.py:117
  614.0 0.4 fusion.55
  614.6 0.3 convolution_bitcast_fusion
  614.9 0.3 copy.45
  615.2 0.2 reshape.110
  615.5 0.3 convolution_bitcast_fusion.1
  615.8 0.3 copy.38
  616.2 0.2 reshape.103
  616.7 1.0 bitcast_multiply_fusion.2
  617.8 0.3 broadcast_in_dim.68
  618.2 1.2 fusion.14
  619.3 247.2 %all-reduce.5.cloned.1.call-done = f32[64,2048]{1,0:T(8,128)} async-done(((f32[64,2048]{1,0:T(8,128)}), f32[64,2048]{1,0:T(8,128)}) %all-reduce.5.cloned.1.call-update) | async-done | bytes 524304 | tf_op jit(solution)/shard_map/psum | solution.py:117
  866.7 0.2 broadcast_in_dim.75
  866.9 0.2 broadcast_in_dim.74
  867.1 2.2 fusion.16
  (58 shorter events, 2.0 us)
Async XLA Ops:
  7.2 4.4 copy-start.1
  7.2 5.3 copy-start
  7.2 5.3 copy-start.10
  7.2 57.1 %all-gather.4.cloned.1.call-start = ((), (), s32[]{:S(2)}) async-start(), calls=%async_computation | async-start | bytes 4325376 | tf_op jit(solution)/shard_map/all_gather | solution.py:86
  7.9 109.5 %all-gather.6.cloned.1.call-start = ((), (), s32[]{:S(2)}) async-start(), calls=%async_computation.1 | async-start | bytes 4325376 | tf_op jit(solution)/shard_map/all_gather | solution.py:87
  8.7 364.9 %all-reduce.3.cloned.1.call-start = ((), (), s32[]{:S(2)}) async-start(), calls=%async_computation.2 | async-start | bytes 524288 | tf_op jit(solution)/shard_map/psum | solution.py:14
  12.5 105.0 %copy-start.3 = (bf16[64,4096]{1,0:T(8,128)(2,1)}, bf16[64,4096]{1,0:T(8,128)(2,1)S(1)}, u32[]{:S(2)}) copy-start(bf16[64,4096]{1,0:T(8,128)(2,1)S(1)} %fusion.11) | copy-start | bytes 1572868
  67.6 54.5 %copy-start.11 = (s32[256]{0:T(256)S(1)}, s32[256]{0:T(256)}, u32[]{:S(2)}) copy-start(s32[256]{0:T(256)} %param.13) | copy-start | bytes 3076
  120.6 331.5 %copy-start.4 = (bf16[64,4096]{1,0:T(8,128)(2,1)S(1)}, bf16[64,4096]{1,0:T(8,128)(2,1)}, u32[]{:S(2)}) copy-start(bf16[64,4096]{1,0:T(8,128)(2,1)} %copy-done.3) | copy-start | bytes 1572868
  121.4 330.7 %all-gather.8.cloned.1.call-start = ((), (), s32[]{:S(2)}) async-start(), calls=%async_computation.3 | async-start | bytes 17301504 | tf_op jit(solution)/shard_map/all_gather | solution.py:85
  122.0 744.5 %all-reduce.5.cloned.1.call-start = ((), (), s32[]{:S(2)}) async-start(), calls=%async_computation.4 | async-start | bytes 1048576 | tf_op jit(solution)/shard_map/psum | solution.py:117
  459.8 0.9 copy-start.2
  460.3 0.9 copy-start.5
  460.3 1.0 copy-start.6
  461.2 1.0 slice-start
  461.7 0.9 copy-start.9
  461.8 152.2 %copy-start.8 = (bf16[64,4,128]{2,1,0:T(4,128)(2,1)S(1)}, bf16[64,4,128]{2,1,0:T(4,128)(2,1)}, u32[]{:S(2)}) copy-start(bf16[64,4,128]{2,1,0:T(4,128)(2,1)} %reshape.106) | copy-start | bytes 196612
  462.1 152.5 %copy-start.7 = (bf16[64,4,128]{2,1,0:T(4,128)(2,1)S(1)}, bf16[64,4,128]{2,1,0:T(4,128)(2,1)}, u32[]{:S(2)}) copy-start(bf16[64,4,128]{2,1,0:T(4,128)(2,1)} %reshape.109) | copy-start | bytes 196612
Sparse Core Ops, SparseCore 0:
  10.6 53.7 all-gather.3
  66.9 50.5 all-gather.5
  123.5 250.0 all-reduce.2
  375.9 76.1 all-gather.7
  617.9 248.6 all-reduce.4
where the time goes:
time: 876 us
  waiting for transfers between devices  674 us (77%)
  blocking collectives  150 us (17%)
  matrix products  16.3 us (2%)
  between operations  14.2 us (2%)
  other arithmetic  11.4 us (1%)
  local copies, waits for them, and re-layouts  9.33 us (1%)
    psum x1, waiting for transfers between devices, per_device(): lax.psum((block_part[1] * rescale, block_part[2] * spread(rescale)), ('ou...  247 us
    psum x1, waiting for transfers between devices, broadcast(): return lax.psum(block, axis)  247 us
    all_gather x1, waiting for transfers between devices, per_device(): lax.all_gather(w_query, 'inner', axis=0, tiled=True)  76.8 us
    pmax x1, blocking collectives, per_device(): highest = lax.pmax(block_part[0], ('outer', 'inner'))  76 us
    psum x1, blocking collectives, per_device(): lax.psum((block_part[1] * rescale, block_part[2] * spread(rescale)), ('ou...  74.4 us
    all_gather x1, waiting for transfers between devices, per_device(): lax.all_gather(w_key, 'inner', axis=0, tiled=True)  51.5 us
    all_gather x1, waiting for transfers between devices, per_device(): lax.all_gather(value_weight, 'inner', axis=0, tiled=True)  49.9 us
  transfers between devices with their start and end apart: 5, of which 5 were waited for; matrix products, arithmetic and copies ran while one was open for 2% of the time, Pallas kernels for 0%

commit v1 on v0

--- a/solution.py
+++ b/solution.py
@@ -114,9 +114,9 @@
     block_part = attend_part(query_q, block_k, block_v, reached)
     highest = lax.pmax(block_part[0], ("outer", "inner"))
     rescale = jnp.exp(block_part[0] - highest)
-    summed_parts = lax.psum(
-        (block_part[1] * rescale, block_part[2] * spread(rescale)), ("outer", "inner")
-    )
+    summed_parts = (block_part[1] * rescale, block_part[2] * spread(rescale))
+    for mesh_axis in ("outer", "inner"):
+        summed_parts = lax.psum(summed_parts, mesh_axis)
     merged = (highest, summed_parts[0], summed_parts[1])
     query_places = jnp.arange(query_count, dtype=jnp.int32)
     self_part = attend_part(

time: 876 us -> 743 us (0.85)
  waiting for transfers between devices: 674 us -> 541 us
    psum x1 -> x2, waiting for transfers between devices: 247 us -> 111 us  [per_device(): summed_parts = lax.psum(summed_parts, mesh_axis)]
    psum x1 -> x2, blocking collectives: 74.4 us -> 75.4 us  [per_device(): summed_parts = lax.psum(summed_parts, mesh_axis)]
  transfers between devices with their start and end apart: 5 -> 6, of which waited for: 5 -> 5; matrix products, arithmetic and copies ran while one was open for 2% -> 2% of each run, Pallas kernels for 0% -> 0%
where the time goes in v1:
time: 743 us; the launch traced here: 741 us
  waiting for transfers between devices  541 us (73%)
  blocking collectives  151 us (20%)
  matrix products  16.4 us (2%)
  between operations  14.5 us (2%)
  other arithmetic  11.5 us (2%)
    psum x1, waiting for transfers between devices, broadcast(): return lax.psum(block, axis)  249 us
    psum x2, waiting for transfers between devices, per_device(): summed_parts = lax.psum(summed_parts, mesh_axis)  111 us
    all_gather x1, waiting for transfers between devices, per_device(): lax.all_gather(w_query, 'inner', axis=0, tiled=True)  77.4 us
    pmax x1, blocking collectives, per_device(): highest = lax.pmax(block_part[0], ('outer', 'inner'))  76 us
    psum x2, blocking collectives, per_device(): summed_parts = lax.psum(summed_parts, mesh_axis)  75.4 us
    all_gather x1, waiting for transfers between devices, per_device(): lax.all_gather(w_key, 'inner', axis=0, tiled=True)  51.5 us
    all_gather x1, waiting for transfers between devices, per_device(): lax.all_gather(value_weight, 'inner', axis=0, tiled=True)  49.9 us
  transfers between devices with their start and end apart: 6, of which 5 were waited for; matrix products, arithmetic and copies ran while one was open for 2% of the time, Pallas kernels for 0%

profile of v1, /device:TPU:2, one launch (start us, length us, event | category | flops | bytes accessed | tf_op | source)
XLA Modules:
  0.0 740.8 jit_solution(17120468076888115843)
XLA Ops:
  7.2 0.7 all-gather.4.cloned.1.call-update
  8.0 0.7 all-gather.6.cloned.1.call-update
  8.7 1.2 fusion.9
  10.0 1.5 fusion
  11.5 0.9 fusion.11
  12.5 0.3 fusion.2
  12.8 51.5 %all-gather.4.cloned.1.call-done = bf16[4096,512]{1,0:T(8,128)(2,1)} async-done(((bf16[128,512]{1,0:T(8,128)(2,1)}), bf16[4096,512]{1,0:T(8,128)(2,1)}) %all-gather.4.cloned.1.call-update) | async-done | bytes 4194320 | tf_op jit(solution)/shard_map/all_gather | solution.py:86
  64.3 3.2 convolution_convert_fusion.2
  67.6 49.9 %all-gather.6.cloned.1.call-done = bf16[4096,512]{1,0:T(8,128)(2,1)} async-done(((bf16[128,512]{1,0:T(8,128)(2,1)}), bf16[4096,512]{1,0:T(8,128)(2,1)}) %all-gather.6.cloned.1.call-update) | async-done | bytes 4194320 | tf_op jit(solution)/shard_map/all_gather | solution.py:87
  117.5 3.2 convolution_convert_fusion.1
  120.7 0.7 maximum_select_fusion
  121.5 0.5 all-gather.8.cloned.1.call-update
  122.1 0.6 fusion.52
  122.7 0.7 compare_and_fusion
  123.3 0.6 iota_compare_fusion.2
  124.3 0.1 copy.28
  124.5 249.0 %all-reduce.4.cloned.1.call-done = bf16[2,128,512]{2,1,0:T(8,128)(2,1)} async-done(((bf16[2,128,512]{2,1,0:T(8,128)(2,1)}), bf16[2,128,512]{2,1,0:T(8,128)(2,1)}) %all-reduce.4.cloned.1.call-update) | async-done | bytes 262160 | tf_op jit(solution)/shard_map/psum | solution.py:14
  373.5 1.0 fusion.49
  374.6 0.1 copy.56
  374.7 77.4 %all-gather.8.cloned.1.call-done = bf16[4096,2048]{1,0:T(8,128)(2,1)} async-done(((bf16[128,2048]{1,0:T(8,128)(2,1)}), bf16[4096,2048]{1,0:T(8,128)(2,1)}) %all-gather.8.cloned.1.call-update) | async-done | bytes 16777232 | tf_op jit(solution)/shard_map/all_gather | solution.py:85
  452.2 7.7 %convolution_convert_fusion = bf16[192,2048]{1,0:T(8,128)(2,1)S(1)} fusion(bf16[4096,2048]{1,0:T(8,128)(2,1)} %all-gather.8.cloned.1.call-done, bf16[64,4096]{1,0:T(8,128)(2,1)S(1)} %fusion.11, bf16[128,4096]{1,0:T(8,128)(2,1)S(1)} %fusion.2), kind=kOutput, calls=%fused_computation.2 | convolution fusion | flops 3224764416 | bytes 19136512 | tf_op jit(solution)/shard_map/dot_general | solution.py:80
  459.9 0.4 reshape.98
  460.3 0.2 reshape.102
  460.5 0.4 fusion.54
  460.9 76.0 %pmax.7 = f32[16,64]{1,0:T(8,128)S(1)} all-reduce(f32[16,64]{1,0:T(8,128)S(1)} %bitcast.97), channel_id=1, replica_groups=mesh['outer'=8,'inner'=32] {'outer','inner'}, use_global_device_ids=true, to_apply=%region_6.7 | all-reduce | flops 1024 | bytes 8192 | tf_op jit(solution)/shard_map/pmax | solution.py:115
  536.9 0.4 fusion.19
  537.3 0.3 convolution_bitcast_fusion.1
  537.6 0.3 copy.38
  538.0 0.2 reshape.103
  538.3 0.2 broadcast_in_dim.71
  538.5 1.0 bitcast_multiply_fusion.2
  539.6 0.5 fusion.53
  540.1 0.3 fusion.3
  540.4 0.5 fusion.12
  540.9 0.4 fusion.55
  541.4 0.3 copy.34
  541.9 16.5 %psum.38 = f32[16,64]{1,0:T(8,128)S(1)} all-reduce(f32[16,64]{1,0:T(8,128)S(1)} %get-tuple-element.13), channel_id=1, replica_groups=mesh['outer'=8,'inner'=32] {'outer'}, use_global_device_ids=true, to_apply=%region_11.12 | all-reduce | flops 1024 | bytes 8192 | tf_op jit(solution)/shard_map/psum | solution.py:119
  558.4 58.9 %psum.39 = f32[16,64]{1,0:T(8,128)S(1)} all-reduce(f32[16,64]{1,0:T(8,128)S(1)} %psum.38), channel_id=1, replica_groups=mesh['outer'=8,'inner'=32] {'inner'}, use_global_device_ids=true, to_apply=%region_12.13 | all-reduce | flops 1024 | bytes 8192 | tf_op jit(solution)/shard_map/psum | solution.py:119
  617.4 0.3 convolution_bitcast_fusion
  617.7 0.3 copy.45
  618.0 0.2 reshape.110
  618.4 0.3 broadcast_in_dim.68
  618.8 1.2 fusion.14
  619.9 111.2 %all-reduce.8.cloned.1.call-done = f32[64,2048]{1,0:T(8,128)} async-done(((f32[64,2048]{1,0:T(8,128)}), f32[64,2048]{1,0:T(8,128)}) %all-reduce.8.cloned.1.call-update) | async-done | bytes 524304 | tf_op jit(solution)/shard_map/psum | solution.py:119
  731.1 0.2 broadcast_in_dim.76
  731.3 0.2 broadcast_in_dim.75
  731.5 0.2 broadcast_in_dim.74
  731.7 2.2 fusion.16
  (45 shorter events, 1.4 us)
Async XLA Ops:
  7.2 4.4 copy-start.1
  7.2 5.3 copy-start
  7.2 5.3 copy-start.2
  7.2 57.1 %all-gather.4.cloned.1.call-start = ((), (), s32[]{:S(2)}) async-start(), calls=%async_computation | async-start | bytes 4325376 | tf_op jit(solution)/shard_map/all_gather | solution.py:86
  7.9 109.5 %all-gather.6.cloned.1.call-start = ((), (), s32[]{:S(2)}) async-start(), calls=%async_computation.1 | async-start | bytes 4325376 | tf_op jit(solution)/shard_map/all_gather | solution.py:87
  8.7 364.9 %all-reduce.4.cloned.1.call-start = ((), (), s32[]{:S(2)}) async-start(), calls=%async_computation.2 | async-start | bytes 524288 | tf_op jit(solution)/shard_map/psum | solution.py:14
  67.6 54.5 %copy-start.3 = (s32[256]{0:T(256)S(1)}, s32[256]{0:T(256)}, u32[]{:S(2)}) copy-start(s32[256]{0:T(256)} %param.13) | copy-start | bytes 3076
  121.4 330.7 %all-gather.8.cloned.1.call-start = ((), (), s32[]{:S(2)}) async-start(), calls=%async_computation.3 | async-start | bytes 17301504 | tf_op jit(solution)/shard_map/all_gather | solution.py:85
  122.0 496.4 %all-reduce.6.cloned.1.call-start = ((), (), s32[]{:S(2)}) async-start(), calls=%async_computation.4 | async-start | bytes 1048576 | tf_op jit(solution)/shard_map/psum | solution.py:119
  539.5 191.5 %all-reduce.8.cloned.1.call-start = ((), (), s32[]{:S(2)}) async-start(), calls=%async_computation.5 | async-start | bytes 1048576 | tf_op jit(solution)/shard_map/psum | solution.py:119
Sparse Core Ops, SparseCore 0:
  10.6 53.7 all-gather.3
  66.9 50.5 all-gather.5
  123.5 250.0 all-reduce.3
  376.0 76.1 all-gather.7
  539.7 70.6 all-reduce.5
  618.6 112.4 all-reduce.7
